TPU v7x, 256 devices: a whole 4x4x8 slice. The times are simulated.
256 devices in a mesh: tile: 64 (over z, x, core), rot: 4 (over y).
Axes of the slice: x: 4, y: 4, z: 8, core: 2. Of those that a mesh axis runs over, the one named last changes fastest.
Arguments:
- tomogram: bfloat16 [2048, 5120], P('tile'), may hold values from -12 to 12
- templates: bfloat16 [16, 110592], P('rot', 'tile'), may hold values from -6 to 6
- valid: int32 [2048, 80], P('tile'), may hold values from 0 to 1, as said below
- quats: float32 [4, 4096], replicated, may hold values from -1 to 1, as said below
- rot_index: int32 [16], P('rot'), may hold values from 0 to 4095
Outputs:
- best: float32 [2048, 5120], P('tile', 'rot')
- evidence: float32 [2048, 5120], P('tile', 'rot')
- moments: float32 [4, 2048, 5120], P(None, 'tile', 'rot')
Inputs may be any that keep to these rules, and one draw needn't show every extreme that they name: `valid`: 1 marks a column (x, y) of voxels inside the lamella. `quats`: each column is a unit quaternion with a non-negative first component.
All inputs are finite; a program needn't handle non-finite values.
Results may differ from a plain program's by a relative error of at most 0.0003.
Values may be sent and summed in bfloat16 or wider, within the bound.
A program may use at most 128 MiB of HBM per device.

v0:
```python
import math
import jax
import jax.numpy as jnp
from jax import lax
from jax.sharding import PartitionSpec as P

TEMPL = 48
HALF = 24
EPSILON = 1e-06
TWO_PI = 2.0 * math.pi


def padded(block, sides, width):
    for axis, dim in sides:
        count = lax.axis_size(axis)
        forward = [(i, i + 1) for i in range(count - 1)]
        backward = [(target, source) for source, target in forward]
        low = lax.ppermute(
            lax.slice_in_dim(block, block.shape[dim] - width, None, axis=dim), axis, forward
        )
        high = lax.ppermute(lax.slice_in_dim(block, 0, width, axis=dim), axis, backward)
        block = jnp.concatenate([low, block, high], axis=dim)
    return block


def twiddle(count_in, shift_in, count_out, shift_out, length, direction, factor):
    row_idx = (jnp.arange(count_in, dtype=jnp.int32) + shift_in)[:, None]
    col_idx = (jnp.arange(count_out, dtype=jnp.int32) + shift_out)[None, :]
    phase_idx = jnp.remainder(row_idx * col_idx, length).astype(jnp.float32)
    angles = phase_idx * jnp.float32(direction * TWO_PI / length)
    real_part = jnp.cos(angles) * factor
    imag_part = jnp.sin(angles) * factor
    upper_half = jnp.stack([real_part, imag_part], axis=1)
    lower_half = jnp.stack([-imag_part, real_part], axis=1)
    return jnp.stack([upper_half, lower_half], axis=0)


def product(formula, left_arr, right_arr):
    return jnp.einsum(
        formula,
        left_arr,
        right_arr,
        precision=lax.Precision.HIGH,
        preferred_element_type=jnp.float32,
    )


def forward(volume, shift, direction, lengths):
    size_x, size_y, size_z = volume.shape
    table_z = twiddle(size_z, shift, lengths[2], 0, lengths[2], direction, 1.0)[0]
    spectrum = product("xyz,zdk->dxyk", volume, table_z)
    spectrum = product(
        "cxyz,cydk->dxkz",
        spectrum,
        twiddle(size_y, shift, lengths[1], 0, lengths[1], direction, 1.0),
    )
    return product(
        "cxyz,cxdk->dkyz",
        spectrum,
        twiddle(size_x, shift, lengths[0], 0, lengths[0], direction, 1.0),
    )


def inverse(spectrum, out_x, out_y, out_z, lengths):
    spectrum = product(
        "cxyz,cxdk->dkyz",
        spectrum,
        twiddle(lengths[0], 0, out_x, HALF, lengths[0], 1, 1.0 / lengths[0]),
    )
    spectrum = product(
        "cxyz,cydk->dxkz",
        spectrum,
        twiddle(lengths[1], 0, out_y, 0, lengths[1], 1, 1.0 / lengths[1]),
    )
    real_table = twiddle(lengths[2], 0, out_z, 0, lengths[2], 1, 1.0 / lengths[2])[:, :, 0]
    return product("cxyz,czk->xyk", spectrum, real_table)


def multiply(first_arr, other_arr):
    return jnp.stack(
        [
            first_arr[0] * other_arr[0] - first_arr[1] * other_arr[1],
            first_arr[0] * other_arr[1] + first_arr[1] * other_arr[0],
        ]
    )


def local(tomogram, templates, valid, quats, rot_index):
    x_cells, voxels = tomogram.shape
    y_cells = valid.shape[1]
    z_cells = voxels // y_cells
    lengths = (x_cells + TEMPL, y_cells + HALF, z_cells + HALF)
    widened = padded(tomogram, (("tile", 0),), HALF)
    slab_spectrum = forward(
        widened.astype(jnp.float32).reshape(x_cells + TEMPL, y_cells, z_cells), 0, -1, lengths
    )
    gathered_bank = lax.all_gather(templates, "tile", axis=1, tiled=True).astype(jnp.float32)
    centred = gathered_bank - jnp.mean(gathered_bank, axis=1, keepdims=True)
    tmpl_spread = jnp.sqrt(jnp.mean(centred * centred, axis=1, keepdims=True) + EPSILON)
    unit_bank = centred / (tmpl_spread * jnp.float32(TEMPL) ** 1.5)

    def correlate(unit_tmpl):
        tmpl_spectrum = forward(unit_tmpl.reshape(TEMPL, TEMPL, TEMPL), -HALF, 1, lengths)
        return inverse(multiply(slab_spectrum, tmpl_spectrum), x_cells, y_cells, z_cells, lengths)

    correlation = lax.map(correlate, unit_bank).reshape(unit_bank.shape[0], x_cells, voxels)
    inside = jnp.repeat(valid.astype(jnp.float32), z_cells, axis=1)
    columns = jnp.sum(valid.astype(jnp.float32))
    masked = correlation * inside[None]
    first_sum, all_columns = lax.psum((jnp.sum(masked, axis=(1, 2)), columns), "tile")
    voxel_count = all_columns * z_cells
    average = first_sum / voxel_count
    deviation = correlation - average[:, None, None]
    square_sum = lax.psum(jnp.sum(inside[None] * deviation * deviation, axis=(1, 2)), "tile")
    spread = jnp.sqrt(square_sum / voxel_count + EPSILON)
    scores = (correlation - average[:, None, None]) / spread[:, None, None]
    one_hot = (rot_index[:, None] == jnp.arange(quats.shape[1], dtype=jnp.int32)[None, :]).astype(
        jnp.float32
    )
    orient = product("rq,kq->rk", one_hot, quats)
    highest = jnp.max(scores, axis=0)
    weight = jnp.exp(scores - highest[None])
    exp_total = jnp.sum(weight, axis=0)
    moment = product("rxv,rk->kxv", weight, orient)
    groups = lax.axis_size("rot")
    share_len = voxels // groups
    offset = lax.axis_index("rot") * share_len
    high_full = lax.pmax(highest, "rot")
    rescale = jnp.exp(highest - high_full)
    total_full, moment_full = lax.psum((exp_total * rescale, moment * rescale[None]), "rot")
    high_all = lax.dynamic_slice_in_dim(high_full, offset, share_len, 1)
    total_all = lax.dynamic_slice_in_dim(total_full, offset, share_len, 1)
    moment_all = lax.dynamic_slice_in_dim(moment_full, offset, share_len, 2)
    inside_part = lax.dynamic_slice_in_dim(inside, offset, share_len, 1)
    best = inside_part * high_all
    evidence = inside_part * (high_all + jnp.log(total_all))
    moments = inside_part[None] * moment_all / total_all[None]
    return (best, evidence, moments)


def solution(mesh):
    placed = (P("tile", None), P("rot", "tile"), P("tile", None), P(), P("rot"))
    return jax.shard_map(
        local,
        mesh=mesh,
        in_specs=placed,
        out_specs=(P("tile", "rot"), P("tile", "rot"), P(None, "tile", "rot")),
        check_vma=False,
    )
```

profile of v0, /device:TPU:1, one launch (start us, length us, event | category | flops | bytes accessed | tf_op | source)
XLA Modules:
  0.0 683.0 jit_solution(3317119279552520776)
XLA Ops:
  7.2 1.8 fusion.124
  9.0 4.5 collective-permute-start
  13.5 1.9 collective-permute-start.1
  16.4 55.7 %all-gather = bf16[64,1728,4]{1,2,0:T(4,128)(2,1)S(1)} all-gather(bf16[1,1728,4]{1,2,0:T(4,128)(2,1)} %bitcast.196), channel_id=1, replica_groups=mesh['tile'=64,'rot'=4] {'tile'}, dimensions={0}, use_global_device_ids=true | all-gather | bytes 898560 | tf_op jit(solution)/shard_map/all_gather | solution.py:97
  74.6 2.8 reshape.771
  78.5 1.6 divide_bitcast_fusion
  82.6 1.5 reshape.767
  84.1 4.6 convolution_bitcast_fusion.1
  88.8 9.4 %copy.71 = f32[2,80,80,88,1]{2,1,0,4,3:T(8,128)} copy(f32[2,80,80,88,1]{3,2,1,0,4:T(8,128)} %convolution_bitcast_fusion.1) | data formatting | bytes 9011200 | tf_op jit(solution)/shard_map/xyz,zdk->dxyk/transpose | solution.py:39
  98.2 5.5 fusion.90
  103.7 5.6 fusion.83
  109.3 145.3 %while.13 = (s32[]{:T(128)}, f32[4,32,80,64]{2,3,1,0:T(8,128)}, f32[2,80,104,88]{2,1,3,0:T(8,128)}, f32[4,110592]{1,0:T(4,128)}, s32[]{:T(128)}) while((s32[]{:T(128)}, f32[4,32,80,64]{2,3,1,0:T(8,128)}, f32[2,80,104,88]{2,1,3,0:T(8,128)}, f32[4,110592]{1,0:T(4,128)}, s32[]{:T(128)}) %tuple.86), condition=%wide.region_3.4_spmd, body=%wide.region_2.3_spmd.sunk | while | flops 2770436608 | bytes 55842368 | solution.py:106
  109.6 2.8 dynamic-slice_reduce_fusion.2
  112.4 1.5 reshape.806
  114.1 2.3 convolution_bitcast_fusion.4
  116.4 4.6 copy.104
  121.0 3.8 fusion.158
  125.1 3.1 fusion.160
  128.1 5.9 multiply_subtract_fusion.2
  134.2 4.5 fusion.161
  139.1 3.5 fusion.163
  143.0 2.7 fusion.165
  145.9 2.8 dynamic-slice_reduce_fusion.2
  148.6 1.5 reshape.806
  150.3 2.3 convolution_bitcast_fusion.4
  152.7 4.6 copy.104
  157.2 3.8 fusion.158
  161.3 3.1 fusion.160
  164.4 5.9 multiply_subtract_fusion.2
  170.5 4.5 fusion.161
  175.4 3.5 fusion.163
  179.2 2.7 fusion.165
  182.1 2.8 dynamic-slice_reduce_fusion.2
  186.6 2.3 convolution_bitcast_fusion.4
  188.9 4.6 copy.104
  193.5 3.8 fusion.158
  197.5 3.1 fusion.160
  200.6 5.9 multiply_subtract_fusion.2
  206.7 4.5 fusion.161
  211.6 3.5 fusion.163
  215.4 2.7 fusion.165
  218.4 2.8 dynamic-slice_reduce_fusion.2
  222.8 2.3 convolution_bitcast_fusion.4
  225.1 4.6 copy.104
  229.7 3.8 fusion.158
  233.8 3.1 fusion.160
  236.8 5.9 multiply_subtract_fusion.2
  242.9 4.5 fusion.161
  247.8 3.5 fusion.163
  251.7 2.7 fusion.165
  254.6 2.8 multiply_reduce_fusion
  257.7 124.2 %all-reduce = (f32[4]{0:T(128)S(1)}, f32[]{:T(128)}) all-reduce(f32[4]{0:T(128)S(1)} %multiply_reduce_fusion, f32[]{:T(128)} %convert_reduce_fusion.1), channel_id=1, replica_groups=mesh['tile'=64,'rot'=4] {'tile'}, use_global_device_ids=true, to_apply=%region_5.6 | all-reduce | flops 5 | bytes 40 | tf_op jit(solution)/shard_map/psum | solution.py:110
  382.6 3.1 fusion.82
  385.7 5.7 copy.55
  391.4 126.6 %psum.37 = f32[4]{0:T(128)S(1)} all-reduce(f32[4]{0:T(128)S(1)} %fusion.82), channel_id=1, replica_groups=mesh['tile'=64,'rot'=4] {'tile'}, use_global_device_ids=true, to_apply=%region_9.10 | all-reduce | flops 4 | bytes 32 | tf_op jit(solution)/shard_map/psum | solution.py:114
  518.1 3.0 fusion.122
  521.5 4.4 exponential_reduce_fusion
  527.1 5.4 reshape.768
  534.2 2.2 subtract_exponential_fusion
  536.5 41.4 %all-reduce.5.cloned.1.call-done = f32[32,5120]{1,0:T(8,128)} async-done(((f32[32,5120]{1,0:T(8,128)}), f32[32,5120]{1,0:T(8,128)}) %all-reduce.5.cloned.1.call-update) | async-done | bytes 655376 | tf_op jit(solution)/shard_map/pmax | solution.py:128
  577.9 2.2 fusion.123
  580.1 5.6 convolution_multiply_fusion
  586.6 85.2 %all-reduce.7.cloned.1.call-done = (f32[32,5120]{1,0:T(8,128)}, f32[4,32,5120]{2,0,1:T(4,128)}) async-done(((f32[32,5120]{1,0:T(8,128)}, f32[4,32,5120]{2,0,1:T(4,128)}), (f32[32,5120]{1,0:T(8,128)}, f32[4,32,5120]{2,0,1:T(4,128)})) %all-reduce.7.cloned.1.call-update) | async-done | bytes 3276816 | tf_op jit(solution)/shard_map/psum | solution.py:130
  671.7 1.8 add_multiply_fusion
  (109 shorter events, 22.4 us)
Async XLA Ops:
  7.2 250.3 %copy-start = (f32[4,4096]{1,0:T(4,128)S(1)}, f32[4,4096]{1,0:T(4,128)}, u32[]{:S(2)}) copy-start(f32[4,4096]{1,0:T(4,128)} %param.10) | copy-start | bytes 196612
  7.2 570.7 %all-reduce.5.cloned.1.call-start = ((), (), s32[]{:S(2)}) async-start(), calls=%async_computation | async-start | bytes 1310720 | tf_op jit(solution)/shard_map/pmax | solution.py:128
  9.0 71.8 %collective-permute-start = (bf16[24,5120]{1,0:T(8,128)(2,1)}, bf16[24,5120]{1,0:T(8,128)(2,1)S(1)}, u32[]{:S(2)}, u32[]{:S(2)}) collective-permute-start(bf16[24,5120]{1,0:T(8,128)(2,1)} %get-tuple-element.138), channel_id=1, source_target_pairs={{0,4},{4,8},{8,12},{12,16},{16,20},{20,24},{24,28},{28,32},{32,36}... | collective-permute-start | bytes 737288 | tf_op jit(solution)/shard_map/ppermute | solution.py:18
  13.5 68.0 %collective-permute-start.1 = (bf16[24,5120]{1,0:T(8,128)(2,1)S(1)}, bf16[24,5120]{1,0:T(8,128)(2,1)}, u32[]{:S(2)}, u32[]{:S(2)}) collective-permute-start(bf16[24,5120]{1,0:T(8,128)(2,1)S(1)} %get-tuple-element.139), channel_id=1, source_target_pairs={{4,0},{8,4},{12,8},{16,12},{20,16},{24,20},{28,24},{32,28},{36,32}... | collective-permute-start | bytes 737288 | tf_op jit(solution)/shard_map/ppermute | solution.py:21
  74.6 5.6 copy-start.5
  77.4 4.1 copy-start.3
  80.8 0.7 copy-start.4
  254.6 2.9 copy-start.6
  527.1 5.4 copy-start.2
  532.5 1.7 copy-start.1
  534.2 137.5 %all-reduce.7.cloned.1.call-start = ((), (), s32[]{:S(2)}) async-start(), calls=%async_computation.1 | async-start | bytes 6553600 | tf_op jit(solution)/shard_map/psum | solution.py:130
Sparse Core Ops, SparseCore 0:
  534.3 43.5 all-reduce.4
  585.9 85.7 all-reduce.6
where the time goes:
time: 690 us; the launch traced here: 683 us
  blocking collectives  307 us (44%)
  waiting for transfers between devices  127 us (18%)
  matrix products  101 us (15%)
  local copies, waits for them, and re-layouts  69.1 us (10%)
  other arithmetic  56.8 us (8%)
  between operations  15.3 us (2%)
    psum x1, blocking collectives, local(): lax.psum(jnp.sum(inside[None] * deviation * deviation, axis=(1, 2)), 'tile')  127 us
    psum x1, blocking collectives, local(): lax.psum((jnp.sum(masked, axis=(1, 2)), columns), 'tile')  124 us
    dot_general x29, matrix products, product(): jnp.einsum(formula, left_arr, right_arr, precision=lax.Precision.HIGH, pr...  101 us
    psum x1, waiting for transfers between devices, local(): lax.psum((exp_total * rescale, moment * rescale[None]), 'rot')  85.2 us
    all_gather x1, blocking collectives, local(): lax.all_gather(templates, 'tile', axis=1, tiled=True).astype(jnp.float32)  55.7 us
    pmax x1, waiting for transfers between devices, local(): high_full = lax.pmax(highest, 'rot')  41.4 us
    transpose x5, local copies, waits for them, and re-layouts, product(): jnp.einsum(formula, left_arr, right_arr, precision=lax.Precision.HIGH, pr...  27.7 us
    sub x4, other arithmetic, multiply(): first_arr[0] * other_arr[0] - first_arr[1] * other_arr[1]  23.7 us
  transfers between devices with their start and end apart: 4, of which 2 were waited for; matrix products, arithmetic and copies ran while one was open for 2% of the time, Pallas kernels for 0%

commit v1 on v0

--- a/solution.py
+++ b/solution.py
@@ -94,7 +94,9 @@
     slab_spectrum = forward(
         widened.astype(jnp.float32).reshape(x_cells + TEMPL, y_cells, z_cells), 0, -1, lengths
     )
-    gathered_bank = lax.all_gather(templates, "tile", axis=1, tiled=True).astype(jnp.float32)
+    gathered_bank = jnp.concatenate(
+        lax.all_to_all(jnp.stack([templates] * lax.axis_size("tile")), "tile", 0, 0), axis=1
+    ).astype(jnp.float32)
     centred = gathered_bank - jnp.mean(gathered_bank, axis=1, keepdims=True)
     tmpl_spread = jnp.sqrt(jnp.mean(centred * centred, axis=1, keepdims=True) + EPSILON)
     unit_bank = centred / (tmpl_spread * jnp.float32(TEMPL) ** 1.5)

time: 690 us -> 660 us (0.957)
  blocking collectives: 307 us -> 253 us
  starting transfers between devices: 6.52 us -> 19.5 us
  loops' own time: 0.79 us -> 12.2 us
  local copies, waits for them, and re-layouts: 69.1 us -> 62.1 us
    all_gather x1 -> x0, blocking collectives: 55.7 us -> none  [local(): lax.all_gather(templates, 'tile', axis=1, tiled=True).astype(jnp.float32)]
    all_to_all x0 -> x1, starting transfers between devices: none -> 13 us  [local(): lax.all_to_all(jnp.stack([templates] * lax.axis_size('tile')), 'tile', 0, 0)]
    another operation x1, loops' own time: 0.79 us -> 12.2 us  [local(): lax.map(correlate, unit_bank).reshape(unit_bank.shape[0], x_cells, voxels)]
  transfers between devices with their start and end apart: 4 -> 5, of which waited for: 2 -> 2; matrix products, arithmetic and copies ran while one was open for 2% -> 5% of each run, Pallas kernels for 0% -> 0%
where the time goes in v1:
time: 660 us; the launch traced here: 649 us
  blocking collectives  253 us (38%)
  waiting for transfers between devices  126 us (19%)
  matrix products  102 us (15%)
  local copies, waits for them, and re-layouts  62.1 us (9%)
  other arithmetic  58.1 us (9%)
  starting transfers between devices  19.5 us (3%)
  between operations  15.3 us (2%)
  loops' own time  12.2 us (2%)
    psum x1, blocking collectives, local(): lax.psum(jnp.sum(inside[None] * deviation * deviation, axis=(1, 2)), 'tile')  129 us
    psum x1, blocking collectives, local(): lax.psum((jnp.sum(masked, axis=(1, 2)), columns), 'tile')  125 us
    dot_general x29, matrix products, product(): jnp.einsum(formula, left_arr, right_arr, precision=lax.Precision.HIGH, pr...  102 us
    psum x1, waiting for transfers between devices, local(): lax.psum((exp_total * rescale, moment * rescale[None]), 'rot')  85.2 us
    pmax x1, waiting for transfers between devices, local(): high_full = lax.pmax(highest, 'rot')  41.1 us
    transpose x5, local copies, waits for them, and re-layouts, product(): jnp.einsum(formula, left_arr, right_arr, precision=lax.Precision.HIGH, pr...  27.7 us
    sub x4, other arithmetic, multiply(): first_arr[0] * other_arr[0] - first_arr[1] * other_arr[1]  23.6 us
  transfers between devices with their start and end apart: 5, of which 2 were waited for; matrix products, arithmetic and copies ran while one was open for 5% of the time, Pallas kernels for 0%

profile of v1, /device:TPU:1, one launch (start us, length us, event | category | flops | bytes accessed | tf_op | source)
XLA Modules:
  0.0 649.0 jit_solution(17571526446893863086)
XLA Ops:
  8.4 4.5 collective-permute-start
  12.9 1.9 collective-permute-start.1
  14.8 1.9 stack.334
  16.7 13.0 %all-to-all-start = ((bf16[64,4,1728]{2,1,0:T(4,128)(2,1)}), bf16[64,4,1728]{2,1,0:T(4,128)(2,1)S(1)}, u32[]{:S(2)}, u32[]{:S(2)}) async-start(bf16[64,4,1728]{2,1,0:T(4,128)(2,1)} %stack.334), calls=%async_computation | async-start | bytes 1835008 | tf_op jit(solution)/shard_map/all_to_all | solution.py:98
  34.4 5.4 convolution_bitcast_fusion.1
  39.8 9.4 %copy.69 = f32[2,80,80,88,1]{2,1,0,4,3:T(8,128)} copy(f32[2,80,80,88,1]{3,2,1,0,4:T(8,128)} %convolution_bitcast_fusion.1) | data formatting | bytes 9011200 | tf_op jit(solution)/shard_map/xyz,zdk->dxyk/transpose | solution.py:39
  49.2 5.5 fusion.92
  54.8 5.6 fusion.83
  63.1 2.6 reshape.780
  65.7 1.8 subtract_divide_fusion.1
  67.6 150.8 %while.13 = (s32[]{:T(128)}, f32[4,32,80,64]{2,3,1,0:T(8,128)}, f32[2,80,104,88]{2,1,3,0:T(8,128)}, f32[4,110592]{1,0:T(4,128)S(1)}, s32[]{:T(128)}) while((s32[]{:T(128)}, f32[4,32,80,64]{2,3,1,0:T(8,128)}, f32[2,80,104,88]{2,1,3,0:T(8,128)}, f32[4,110592]{1,0:T(4,128)S(1)}, s32[]{:T(128)}) %tuple.86), condition=%wide.region_3.4_spmd, body=%wide.region_2.3_spmd.sunk | while | flops 2770436608 | bytes 69998200 | solution.py:108
  79.5 1.3 dynamic-slice_reduce_fusion.2
  80.7 1.5 reshape.815
  82.4 2.3 convolution_bitcast_fusion.4
  84.8 4.6 copy.102
  89.4 3.8 fusion.160
  93.4 3.1 fusion.162
  96.5 5.9 multiply_subtract_fusion.2
  102.6 4.5 fusion.163
  107.5 3.5 fusion.165
  111.3 2.7 fusion.167
  114.2 1.3 dynamic-slice_reduce_fusion.2
  115.5 1.5 reshape.815
  117.2 2.3 convolution_bitcast_fusion.4
  119.5 4.6 copy.102
  124.1 3.8 fusion.160
  128.2 3.1 fusion.162
  131.2 5.9 multiply_subtract_fusion.2
  137.3 4.5 fusion.163
  142.2 3.5 fusion.165
  146.1 2.7 fusion.167
  150.3 1.5 reshape.815
  152.0 2.3 convolution_bitcast_fusion.4
  154.3 4.6 copy.102
  158.9 3.8 fusion.160
  163.0 3.1 fusion.162
  166.0 5.9 multiply_subtract_fusion.2
  172.1 4.5 fusion.163
  177.0 3.5 fusion.165
  180.9 2.7 fusion.167
  185.1 1.5 reshape.815
  186.8 2.3 convolution_bitcast_fusion.4
  189.1 4.6 copy.102
  193.7 3.8 fusion.160
  197.8 3.1 fusion.162
  200.8 5.9 multiply_subtract_fusion.2
  206.9 4.5 fusion.163
  211.8 3.5 fusion.165
  215.7 2.7 fusion.167
  218.4 2.8 multiply_reduce_fusion
  221.5 124.6 %all-reduce = (f32[4]{0:T(128)S(1)}, f32[]{:T(128)}) all-reduce(f32[4]{0:T(128)S(1)} %multiply_reduce_fusion, f32[]{:T(128)} %convert_reduce_fusion.1), channel_id=1, replica_groups=mesh['tile'=64,'rot'=4] {'tile'}, use_global_device_ids=true, to_apply=%region_5.6 | all-reduce | flops 5 | bytes 40 | tf_op jit(solution)/shard_map/psum | solution.py:112
  346.8 3.1 fusion.82
  349.9 5.7 copy.53
  355.6 128.7 %psum.37 = f32[4]{0:T(128)S(1)} all-reduce(f32[4]{0:T(128)S(1)} %fusion.82), channel_id=1, replica_groups=mesh['tile'=64,'rot'=4] {'tile'}, use_global_device_ids=true, to_apply=%region_9.10 | all-reduce | flops 4 | bytes 32 | tf_op jit(solution)/shard_map/psum | solution.py:116
  484.3 3.0 fusion.124
  487.7 4.4 exponential_reduce_fusion
  493.4 5.4 reshape.779
  500.5 2.2 subtract_exponential_fusion
  502.8 41.1 %all-reduce.5.cloned.1.call-done = f32[32,5120]{1,0:T(8,128)} async-done(((f32[32,5120]{1,0:T(8,128)}), f32[32,5120]{1,0:T(8,128)}) %all-reduce.5.cloned.1.call-update) | async-done | bytes 655376 | tf_op jit(solution)/shard_map/pmax | solution.py:130
  543.9 2.2 fusion.125
  546.1 5.6 convolution_multiply_fusion
  552.6 85.2 %all-reduce.7.cloned.1.call-done = (f32[32,5120]{1,0:T(8,128)}, f32[4,32,5120]{2,0,1:T(4,128)}) async-done(((f32[32,5120]{1,0:T(8,128)}, f32[4,32,5120]{2,0,1:T(4,128)}), (f32[32,5120]{1,0:T(8,128)}, f32[4,32,5120]{2,0,1:T(4,128)})) %all-reduce.7.cloned.1.call-update) | async-done | bytes 3276816 | tf_op jit(solution)/shard_map/psum | solution.py:132
  637.7 1.8 add_multiply_fusion
  639.5 1.3 multiply_divide_fusion
  (132 shorter events, 22.2 us)
Async XLA Ops:
  7.2 214.1 %copy-start = (f32[4,4096]{1,0:T(4,128)S(1)}, f32[4,4096]{1,0:T(4,128)}, u32[]{:S(2)}) copy-start(f32[4,4096]{1,0:T(4,128)} %param.10) | copy-start | bytes 196612
  7.2 26.1 %copy-start.5 = (bf16[32,5120]{1,0:T(8,128)(2,1)S(1)}, bf16[32,5120]{1,0:T(8,128)(2,1)}, u32[]{:S(2)}) copy-start(bf16[32,5120]{1,0:T(8,128)(2,1)} %param.7) | copy-start | bytes 983044
  7.2 24.1 %copy-start.9 = (s32[32,80]{1,0:T(8,128)S(1)}, s32[32,80]{1,0:T(8,128)}, u32[]{:S(2)}) copy-start(s32[32,80]{1,0:T(8,128)} %param.9) | copy-start | bytes 30724
  8.4 24.9 %collective-permute-start = (bf16[24,5120]{1,0:T(8,128)(2,1)S(1)}, bf16[24,5120]{1,0:T(8,128)(2,1)S(1)}, u32[]{:S(2)}, u32[]{:S(2)}) collective-permute-start(bf16[24,5120]{1,0:T(8,128)(2,1)S(1)} %get-tuple-element.138), channel_id=1, source_target_pairs={{0,4},{4,8},{8,12},{12,16},{16,20},{20,24},{24,28},{28,32},{32,36}... | collective-permute-start | bytes 737288 | tf_op jit(solution)/shard_map/ppermute | solution.py:18
  12.9 20.4 %collective-permute-start.1 = (bf16[24,5120]{1,0:T(8,128)(2,1)S(1)}, bf16[24,5120]{1,0:T(8,128)(2,1)S(1)}, u32[]{:S(2)}, u32[]{:S(2)}) collective-permute-start(bf16[24,5120]{1,0:T(8,128)(2,1)S(1)} %get-tuple-element.139), channel_id=1, source_target_pairs={{4,0},{8,4},{12,8},{16,12},{20,16},{24,20},{28,24},{32,28},{36,32}... | collective-permute-start | bytes 737288 | tf_op jit(solution)/shard_map/ppermute | solution.py:21
  16.7 43.7 %all-to-all-start = ((bf16[64,4,1728]{2,1,0:T(4,128)(2,1)}), bf16[64,4,1728]{2,1,0:T(4,128)(2,1)S(1)}, u32[]{:S(2)}, u32[]{:S(2)}) async-start(bf16[64,4,1728]{2,1,0:T(4,128)(2,1)} %stack.334), calls=%async_computation | async-start | bytes 1835008 | tf_op jit(solution)/shard_map/all_to_all | solution.py:98
  29.7 514.2 %all-reduce.5.cloned.1.call-start = ((), (), s32[]{:S(2)}) async-start(), calls=%async_computation.1 | async-start | bytes 1310720 | tf_op jit(solution)/shard_map/pmax | solution.py:130
  39.8 9.4 %copy-start.6 = (f32[1,80,2,104]{3,1,0,2:T(8,128)S(1)}, f32[1,80,2,104]{3,1,0,2:T(8,128)}, u32[]{:S(2)}) copy-start(f32[1,80,2,104]{3,1,0,2:T(8,128)} %get-tuple-element.143) | copy-start | bytes 199684
  49.2 5.6 copy-start.7
  49.2 5.6 copy-start.8
  79.2 3.2 copy-start.2
  107.5 6.5 %copy-start.3 = (f32[4,110592]{1,0:T(4,128)S(1)}, f32[4,110592]{1,0:T(4,128)}, u32[]{:S(2)}) copy-start(f32[4,110592]{1,0:T(4,128)} %copy-done.2) | copy-start | bytes 5308420 | tf_op jit(solution)/shard_map/while
  114.0 3.2 copy-start.2
  142.2 6.6 %copy-start.3 = (f32[4,110592]{1,0:T(4,128)S(1)}, f32[4,110592]{1,0:T(4,128)}, u32[]{:S(2)}) copy-start(f32[4,110592]{1,0:T(4,128)} %copy-done.2) | copy-start | bytes 5308420 | tf_op jit(solution)/shard_map/while
  148.8 3.2 copy-start.2
  177.0 6.6 %copy-start.3 = (f32[4,110592]{1,0:T(4,128)S(1)}, f32[4,110592]{1,0:T(4,128)}, u32[]{:S(2)}) copy-start(f32[4,110592]{1,0:T(4,128)} %copy-done.2) | copy-start | bytes 5308420 | tf_op jit(solution)/shard_map/while
  183.6 3.2 copy-start.2
  211.8 6.6 %copy-start.3 = (f32[4,110592]{1,0:T(4,128)S(1)}, f32[4,110592]{1,0:T(4,128)}, u32[]{:S(2)}) copy-start(f32[4,110592]{1,0:T(4,128)} %copy-done.2) | copy-start | bytes 5308420 | tf_op jit(solution)/shard_map/while
  218.4 2.9 copy-start.10
  493.4 5.4 copy-start.4
  498.8 1.7 copy-start.1
  500.5 137.3 %all-reduce.7.cloned.1.call-start = ((), (), s32[]{:S(2)}) async-start(), calls=%async_computation.2 | async-start | bytes 6553600 | tf_op jit(solution)/shard_map/psum | solution.py:132
Sparse Core Ops, SparseCore 0:
  500.6 43.2 all-reduce.4
  551.9 85.7 all-reduce.6
